TPU v7x, 512 devices: a whole 4x8x8 slice. The times are simulated.
512 devices in a mesh: grp: 16 (over z, core), blk: 32 (over y, x).
Axes of the slice: x: 4, y: 8, z: 8, core: 2. Of those that a mesh axis runs over, the one named last changes fastest.
Arguments:
- integrals: bfloat16 [32, 2048, 2048], P('blk', None, 'grp'), as said below
- tile_mask: int32 [16, 16], replicated, may hold values from 0 to 1, as said below
- tile_owner: int32 [16], replicated, may hold values from 0 to 15, as said below
- occupied_tiles: bfloat16 [16384, 128], P(('grp', 'blk')), may hold values from -0.1875 to 0.1875
- occupied_offsets: int32 [8], replicated, may hold values from 0 to 15, as said below
- virtual_tiles: bfloat16 [16384, 128], P(('grp', 'blk')), may hold values from -0.1875 to 0.1875
- virtual_offsets: int32 [8], replicated, may hold values from 0 to 15, as said below
Outputs:
- polarizability: float32 [32, 32], P('blk')
Inputs may be any that keep to these rules, and one draw needn't show every extreme that they name: `integrals`: after column slot s is placed at basis tile tile_owner[s], the tensor is symmetric in its two basis indices. `tile_mask`: symmetric, with ones on the diagonal. `tile_owner`: each tile exactly once. `occupied_offsets`: 8 different tile offsets, among them 0 and 15. `virtual_offsets`: 8 different tile offsets, among them 0 and 15.
All inputs are finite; a program needn't handle non-finite values.
Results may differ from a plain program's by a relative error of at most 0.004.
Values may be sent and summed in bfloat16 or wider, within the bound.
A program may use at most 64 MiB of HBM per device.

v0:
```python
import jax
import jax.numpy as jnp
from jax import lax
from jax.sharding import PartitionSpec as P

NT = 16


def body(
    integrals,
    tile_mask,
    tile_owner,
    occupied_tiles,
    occupied_offsets,
    virtual_tiles,
    virtual_offsets,
):
    aux_local, basis_size, local_width = integrals.shape
    tile_width = basis_size // NT
    kcount = occupied_offsets.shape[0]
    local_tiles = local_width // tile_width
    group_index = lax.axis_index("grp")
    local_owner = lax.dynamic_slice_in_dim(tile_owner, group_index * local_tiles, local_tiles)
    matches = (local_owner[None, :, None] == jnp.arange(NT, dtype=jnp.int32)[None, None, :]).astype(
        jnp.int32
    )
    column_mask = jnp.sum(tile_mask[:, None, :] * matches, axis=2)
    blocked = integrals.reshape(aux_local, NT, tile_width, local_tiles, tile_width)
    masked = blocked * column_mask.astype(jnp.bfloat16)[None, :, None, :, None]
    masked = masked.reshape(aux_local, NT, tile_width, local_width)
    occupied_all, virtual_all = (
        lax.all_gather(occupied_tiles, ("grp", "blk"), axis=0, tiled=True),
        lax.all_gather(virtual_tiles, ("grp", "blk"), axis=0, tiled=True),
    )
    occupied_all = occupied_all.reshape(NT, kcount, tile_width, tile_width)
    virtual_all = virtual_all.reshape(NT, kcount, tile_width, tile_width)
    source_rows = (tile_owner[:, None] - occupied_offsets[None, :]) % NT
    partner_rows = (tile_owner[:, None] + virtual_offsets[None, :]) % NT
    virtual_pick = virtual_all[tile_owner]
    occupied_sum = jnp.zeros((aux_local, NT, tile_width, local_width), jnp.float32)
    virtual_sum = jnp.zeros((aux_local, local_width, NT, tile_width), jnp.float32)
    for slot in range(kcount):
        occupied_pick = occupied_all[source_rows[:, slot], slot]
        occupied_inputs = masked[:, source_rows[:, slot]]
        occupied_sum = occupied_sum + jnp.einsum(
            "tmn,ptml->ptnl", occupied_pick, occupied_inputs, preferred_element_type=jnp.float32
        )
        virtual_inputs = masked[:, partner_rows[:, slot]]
        virtual_sum = virtual_sum + jnp.einsum(
            "tnm,ptml->pltn",
            virtual_pick[:, slot],
            virtual_inputs,
            preferred_element_type=jnp.float32,
        )
    occupied_part = occupied_sum.astype(jnp.bfloat16)
    virtual_part = virtual_sum.astype(jnp.bfloat16).reshape(
        aux_local, local_tiles, tile_width, basis_size
    )
    occupied_moved = lax.all_to_all(occupied_part, "grp", split_axis=1, concat_axis=3, tiled=True)
    occupied_full, virtual_full = (
        lax.all_to_all(occupied_moved, "blk", split_axis=2, concat_axis=0, tiled=True),
        lax.all_to_all(virtual_part, "blk", split_axis=2, concat_axis=0, tiled=True),
    )
    left_side = occupied_full.reshape(occupied_full.shape[0], -1)
    right_side = virtual_full.reshape(virtual_full.shape[0], -1)
    partial_sum = jnp.einsum(
        "pe,qe->pq", left_side, right_side, preferred_element_type=jnp.float32
    ) * (1.0 / basis_size)
    total = lax.psum(partial_sum, ("grp", "blk"))
    return lax.dynamic_slice_in_dim(total, lax.axis_index("blk") * aux_local, aux_local, 0)


def solution(mesh):
    in_specs = (
        P("blk", None, "grp"),
        P(),
        P(),
        P(("grp", "blk"), None),
        P(),
        P(("grp", "blk"), None),
        P(),
    )
    out_specs = P("blk", None)
    return jax.shard_map(body, mesh=mesh, in_specs=in_specs, out_specs=out_specs, check_vma=False)
```

profile of v0, /device:TPU:1, one launch (start us, length us, event | category | flops | bytes accessed | tf_op | source)
XLA Modules:
  0.0 427.2 jit_solution(16286854891178512670)
XLA Ops:
  34.0 102.1 %all-gather.3.cloned.1.call-done = bf16[16384,128]{1,0:T(8,128)(2,1)} async-done(((bf16[32,128]{1,0:T(8,128)(2,1)}), bf16[16384,128]{1,0:T(8,128)(2,1)}) %all-gather.3.cloned.1.call-update) | async-done | bytes 4194320 | tf_op jit(solution)/shard_map/all_gather | solution.py:32
  136.1 3.6 gather_fusion.1
  139.7 3.6 gather_fusion.3
  143.3 3.6 gather_fusion.5
  146.9 3.6 gather_fusion.7
  150.5 2.9 gather_fusion.9
  153.4 2.8 gather_fusion.11
  156.2 2.8 gather_fusion.13
  159.1 2.8 gather_fusion.15
  162.0 1.7 fusion.25
  163.7 1.6 convolution_add_fusion.13
  168.3 6.0 %all-to-all-start = ((bf16[1,16,128,128]{2,3,0,1:T(8,128)(2,1)}), bf16[1,16,128,128]{2,3,0,1:T(8,128)(2,1)S(1)}, u32[]{:S(2)}, u32[]{:S(2)}) async-start(bf16[1,16,128,128]{2,3,0,1:T(8,128)(2,1)} %fusion.2), calls=%async_computation | async-start | bytes 1048576 | tf_op jit(solution)/shard_map/all_to_all | solution.py:59
  174.4 81.7 %all-gather.5.cloned.1.call-done = bf16[16384,128]{1,0:T(8,128)(2,1)} async-done(((bf16[32,128]{1,0:T(8,128)(2,1)}), bf16[16384,128]{1,0:T(8,128)(2,1)}) %all-gather.5.cloned.1.call-update) | async-done | bytes 4194320 | tf_op jit(solution)/shard_map/all_gather | solution.py:33
  256.1 5.4 %gather_fusion.17 = bf16[16,8,128,128]{3,2,1,0:T(8,128)(2,1)} fusion(bf16[16,8,128,128]{3,2,1,0:T(8,128)(2,1)} %bitcast.152, s32[1024]{0:T(1024)S(1)} %pad_clamp_fusion.8), kind=kCustom, calls=%fused_computation.17 | custom fusion | bytes 8388672 | tf_op jit(solution)/shard_map/gather | solution.py:39
  262.9 1.6 convolution_add_fusion.6
  268.0 3.7 reduce.6
  272.9 6.9 %all-to-all-start.2 = ((bf16[32,2,4096]{2,1,0:T(2,128)(2,1)}), bf16[32,2,4096]{2,1,0:T(2,128)(2,1)S(1)}, u32[]{:S(2)}, u32[]{:S(2)}) async-start(bf16[32,2,4096]{2,1,0:T(2,128)(2,1)} %reshape.405), calls=%async_computation.2 | async-start | bytes 1048576 | tf_op jit(solution)/shard_map/all_to_all | solution.py:62
  280.7 3.7 reduce.7
  285.6 10.8 %all-to-all-done.2 = bf16[32,2,4096]{2,1,0:T(2,128)(2,1)S(1)} async-done(((bf16[32,2,4096]{2,1,0:T(2,128)(2,1)}), bf16[32,2,4096]{2,1,0:T(2,128)(2,1)S(1)}, u32[]{:S(2)}, u32[]{:S(2)}) %all-to-all-start.2) | async-done | bytes 524320 | tf_op jit(solution)/shard_map/all_to_all | solution.py:62
  296.4 5.2 %all-to-all-start.1 = ((bf16[32,2,4096]{2,1,0:T(2,128)(2,1)}), bf16[32,2,4096]{2,1,0:T(2,128)(2,1)S(1)}, u32[]{:S(2)}, u32[]{:S(2)}) async-start(bf16[32,2,4096]{2,1,0:T(2,128)(2,1)} %reshape.407), calls=%async_computation.1 | async-start | bytes 1048576 | tf_op jit(solution)/shard_map/all_to_all | solution.py:61
  302.2 3.0 bitcast_reduce_fusion.1
  305.4 11.3 %all-to-all-done.1 = bf16[32,2,4096]{2,1,0:T(2,128)(2,1)S(1)} async-done(((bf16[32,2,4096]{2,1,0:T(2,128)(2,1)}), bf16[32,2,4096]{2,1,0:T(2,128)(2,1)S(1)}, u32[]{:S(2)}, u32[]{:S(2)}) %all-to-all-start.1) | async-done | bytes 524320 | tf_op jit(solution)/shard_map/all_to_all | solution.py:61
  317.2 3.0 bitcast_reduce_fusion
  321.6 98.2 %psum.7 = f32[32,32]{1,0:T(8,128)S(1)} all-reduce(f32[32,32]{1,0:T(8,128)S(1)} %fusion.3), channel_id=1, replica_groups=mesh['grp'=16,'blk'=32] {'grp','blk'}, use_global_device_ids=true, to_apply=%region_1.2 | all-reduce | flops 1024 | bytes 8192 | tf_op jit(solution)/shard_map/psum | solution.py:69
  (95 shorter events, 41.7 us)
Async XLA Ops:
  6.5 129.6 %all-gather.3.cloned.1.call-start = ((), (), s32[]{:S(2)}) async-start(), calls=%async_computation.3 | async-start | bytes 4202496 | tf_op jit(solution)/shard_map/all_gather | solution.py:32
  7.3 248.8 %all-gather.5.cloned.1.call-start = ((), (), s32[]{:S(2)}) async-start(), calls=%async_computation.4 | async-start | bytes 4202496 | tf_op jit(solution)/shard_map/all_gather | solution.py:33
  23.3 10.7 %copy-start.15 = (s32[16]{0:T(128)S(1)}, s32[16]{0:T(128)}, u32[]{:S(2)}) copy-start(s32[16]{0:T(128)} %param.9) | copy-start | bytes 196
  161.9 3.4 copy-start.2
  161.9 3.4 copy-start.11
  161.9 3.7 copy-start.1
  161.9 3.7 copy-start.10
  163.7 2.4 copy-start.13
  165.3 1.1 copy-start.12
  165.7 1.1 copy-start.14
  168.3 104.6 %all-to-all-start = ((bf16[1,16,128,128]{2,3,0,1:T(8,128)(2,1)}), bf16[1,16,128,128]{2,3,0,1:T(8,128)(2,1)S(1)}, u32[]{:S(2)}, u32[]{:S(2)}) async-start(bf16[1,16,128,128]{2,3,0,1:T(8,128)(2,1)} %fusion.2), calls=%async_computation | async-start | bytes 1048576 | tf_op jit(solution)/shard_map/all_to_all | solution.py:59
  256.1 5.4 %copy-start.3 = (bf16[16,128,128]{2,1,0:T(8,128)(2,1)S(1)}, bf16[16,128,128]{2,1,0:T(8,128)(2,1)}, u32[]{:S(2)}) copy-start(bf16[16,128,128]{2,1,0:T(8,128)(2,1)} %gather_fusion.16) | copy-start | bytes 1572868
  256.1 6.9 %copy-start.4 = (bf16[16,128,128]{2,1,0:T(8,128)(2,1)S(1)}, bf16[16,128,128]{2,1,0:T(8,128)(2,1)}, u32[]{:S(2)}) copy-start(bf16[16,128,128]{2,1,0:T(8,128)(2,1)} %gather_fusion.18) | copy-start | bytes 1572868
  261.4 3.1 copy-start
  261.4 3.1 copy-start.5
  261.4 3.4 copy-start.6
  262.9 2.2 copy-start.7
  264.5 1.1 copy-start.8
  264.8 1.1 copy-start.9
  272.9 23.5 %all-to-all-start.2 = ((bf16[32,2,4096]{2,1,0:T(2,128)(2,1)}), bf16[32,2,4096]{2,1,0:T(2,128)(2,1)S(1)}, u32[]{:S(2)}, u32[]{:S(2)}) async-start(bf16[32,2,4096]{2,1,0:T(2,128)(2,1)} %reshape.405), calls=%async_computation.2 | async-start | bytes 1048576 | tf_op jit(solution)/shard_map/all_to_all | solution.py:62
  296.4 20.3 %all-to-all-start.1 = ((bf16[32,2,4096]{2,1,0:T(2,128)(2,1)}), bf16[32,2,4096]{2,1,0:T(2,128)(2,1)S(1)}, u32[]{:S(2)}, u32[]{:S(2)}) async-start(bf16[32,2,4096]{2,1,0:T(2,128)(2,1)} %reshape.407), calls=%async_computation.1 | async-start | bytes 1048576 | tf_op jit(solution)/shard_map/all_to_all | solution.py:61
Sparse Core Ops, SparseCore 0:
  11.5 124.5 all-gather.2
  140.3 115.6 all-gather.4
where the time goes:
time: 428 us; the launch traced here: 427 us
  waiting for transfers between devices  207 us (48%)
  blocking collectives  98.2 us (23%)
  local copies, waits for them, and re-layouts  66.5 us (16%)
  starting transfers between devices  18.1 us (4%)
  between operations  13.9 us (3%)
  matrix products  12.2 us (3%)
  other arithmetic  10.9 us (3%)
    all_gather x1, waiting for transfers between devices, body(): lax.all_gather(occupied_tiles, ('grp', 'blk'), axis=0, tiled=True)  102 us
    psum x1, blocking collectives, body(): total = lax.psum(partial_sum, ('grp', 'blk'))  98.2 us
    all_gather x1, waiting for transfers between devices, body(): lax.all_gather(virtual_tiles, ('grp', 'blk'), axis=0, tiled=True)  81.7 us
    gather x8, local copies, waits for them, and re-layouts, body(): occupied_pick = occupied_all[source_rows[:, slot], slot]  25.8 us
    all_to_all x1, waiting for transfers between devices, body(): lax.all_to_all(occupied_moved, 'blk', split_axis=2, concat_axis=0, tiled=...  11.3 us
    all_to_all x1, waiting for transfers between devices, body(): lax.all_to_all(virtual_part, 'blk', split_axis=2, concat_axis=0, tiled=True)  10.8 us
    gather x8, local copies, waits for them, and re-layouts, body(): occupied_inputs = masked[:, source_rows[:, slot]]  10.6 us
    gather x8, local copies, waits for them, and re-layouts, body(): virtual_inputs = masked[:, partner_rows[:, slot]]  10.6 us
  transfers between devices with their start and end apart: 5, of which 4 were waited for; matrix products, arithmetic and copies ran while one was open for 20% of the time, Pallas kernels for 0%

commit v1 on v0

v1 whole, which is shorter than its diff:
```python
import functools

import jax
import jax.numpy as jnp
from jax import lax
from jax.experimental import pallas as pl
from jax.experimental.pallas import tpu as pltpu
from jax.sharding import PartitionSpec as P

MESH = pl.DeviceIdType.MESH
TW = 128
F32 = jnp.float32
BF16 = jnp.bfloat16


class Dims:
    def __init__(self, ng, nb, x, kcount):
        self.C = 2
        self.NG, self.NB = ng, nb
        self.Z, self.X, self.Y = ng // 2, x, nb // x
        self.NT, self.K = ng, kcount
        self.RPD = kcount * TW // nb
        self.CH = ng * TW // nb
        self.HP = TW // self.CH


def ring_plan(n, nsub):
    plan = []
    for k in range(1, n // 2 + 1):
        for sub in range(nsub):
            last = 2 * k == n
            if not last:
                plan += [(1, k, sub), (-1, k, sub)]
            else:
                plan.append((1 if sub < (nsub + 1) // 2 else -1, k, sub))
    return plan


class Sems:
    def __init__(self):
        self.count = 0

    def take(self, n=1):
        base = self.count
        self.count += n
        return base


def layout(d, nsub):
    s = Sems()
    t = {}
    for name in ("o", "v"):
        t["x" + name] = s.take(d.X)
    mid = {"o": d.Y, "v": d.Z}
    last = {"o": d.Z, "v": d.Y}
    for name in ("o", "v"):
        t["mid" + name] = {e: s.take() for e in ring_plan(mid[name], 1)}
        t["last" + name] = {e: s.take() for e in ring_plan(last[name], nsub)}
        t["sib" + name] = {e: s.take() for e in ring_plan(last[name], nsub)}
        t["own" + name] = s.take()
    t["R"] = s.take(d.NB)
    t["Lg"] = s.take(d.NG)
    t["Lb"] = s.take(d.NB)
    t["S1"] = s.take(d.NB)
    t["S2"] = s.take(d.NG)
    return t, s.count


def kernel(
    d,
    nsub,
    t,
    mask_ref,
    owner_ref,
    ooff_ref,
    voff_ref,
    b_ref,
    ot_ref,
    vt_ref,
    out_ref,
    go,
    gv,
    bm,
    bt,
    rbuf,
    rb,
    lbuf,
    lg,
    lb,
    s1,
    s1r,
    s2,
    ssem,
    rsem,
):
    g = lax.axis_index("grp")
    b = lax.axis_index("blk")
    z, c = g // 2, lax.rem(g, 2)
    y, x = b // d.X, lax.rem(b, d.X)
    sib = z * 2 + (1 - c)

    def rcopy(src, dst, i, j, gg, bb):
        return pltpu.make_async_remote_copy(
            src_ref=src,
            dst_ref=dst,
            send_sem=ssem.at[i],
            recv_sem=rsem.at[j],
            device_id=(gg, bb),
            device_id_type=MESH,
        )

    barrier = pltpu.get_barrier_semaphore()

    @pl.loop(1, d.NG)
    def _(k):
        pl.semaphore_signal(
            barrier, inc=1, device_id=(lax.rem(g + k, d.NG), b), device_id_type=MESH
        )

    @pl.loop(1, d.NB)
    def _(k):
        pl.semaphore_signal(
            barrier, inc=1, device_id=(g, lax.rem(b + k, d.NB)), device_id_type=MESH
        )

    go[z, c, y, x] = ot_ref[...]
    gv[z, c, y, x] = vt_ref[...]
    pl.semaphore_wait(barrier, d.NG + d.NB - 2)

    bufs = {"o": go, "v": gv}
    sends = []

    for k in range(1, d.X):
        for name in ("o", "v"):
            ref = bufs[name].at[z, c, y, x]
            i = t["x" + name] + k
            cp = rcopy(ref, ref, i, i, g, y * d.X + lax.rem(x + k, d.X))
            cp.start()
            sends.append(cp)

    own = owner_ref[g]

    @pl.loop(0, d.NT)
    def _(i):
        m = mask_ref[i, own].astype(F32)
        tile = (b_ref[0, pl.ds(pl.multiple_of(i * TW, TW), TW), :].astype(F32) * m).astype(BF16)
        bm[i] = tile
        bt[i] = tile.T

    for k in range(1, d.X):
        for name in ("o", "v"):
            ref = bufs[name].at[z, c, y, lax.rem(x - k + d.X, d.X)]
            i = t["x" + name] + k
            rcopy(ref, ref, i, i, g, b).wait_recv()

    def along_z(k):
        return lax.rem(z + k + d.Z, d.Z) * 2 + c, b

    def along_y(k):
        return g, lax.rem(y + k + d.Y, d.Y) * d.X + x

    def pos_z(k):
        return lax.rem(z + k + d.Z, d.Z)

    def pos_y(k):
        return lax.rem(y + k + d.Y, d.Y)

    def mid_block(name, off):
        if name == "o":
            return go.at[z, c, pos_y(off)]
        return gv.at[pos_z(off), c, y]

    def last_block(name, off, sub, core):
        if name == "o":
            h = d.Y // nsub
            return go.at[pos_z(off), core, pl.ds(sub * h, h)]
        h = d.Z // nsub
        return gv.at[pl.ds(sub * h, h), core, pos_y(off)]

    mid_axis = {"o": along_y, "v": along_z}
    last_axis = {"o": along_z, "v": along_y}

    def run(stage, sizes, axis, block, nsubs, forward):
        plans = {name: ring_plan(sizes[name], nsubs) for name in ("o", "v")}

        def send(name, e):
            dirn, k, sub = e
            ref = block(name, -dirn * (k - 1), sub)
            i = t[stage + name][e]
            cp = rcopy(ref, ref, i, i, *axis[name](dirn))
            cp.start()
            sends.append(cp)

        for name in ("o", "v"):
            for e in plans[name]:
                if e[1] == 1:
                    send(name, e)
        if forward:
            for name in ("o", "v"):
                forward(name, None)
        order = []
        for n in range(max(len(plans["o"]), len(plans["v"]))):
            for name in ("v", "o"):
                if n < len(plans[name]):
                    order.append((name, plans[name][n]))
        for name, e in order:
            dirn, k, sub = e
            ref = block(name, -dirn * k, sub)
            i = t[stage + name][e]
            rcopy(ref, ref, i, i, g, b).wait_recv()
            nxt = (dirn, k + 1, sub)
            if nxt in plans[name]:
                send(name, nxt)
            if forward:
                forward(name, e)

    def sibling(name, e):
        if e is None:
            ref = go.at[z, c] if name == "o" else gv.at[:, c, y]
            i = t["own" + name]
        else:
            dirn, k, sub = e
            ref = last_block(name, -dirn * k, sub, c)
            i = t["sib" + name][e]
        cp = rcopy(ref, ref, i, i, sib, b)
        cp.start()
        sends.append(cp)

    def from_sibling(name):
        ref = go.at[z, 1 - c] if name == "o" else gv.at[:, 1 - c, y]
        i = t["own" + name]
        rcopy(ref, ref, i, i, g, b).wait_recv()
        n = d.Z if name == "o" else d.Y
        for e in ring_plan(n, nsub):
            dirn, k, sub = e
            ref = last_block(name, -dirn * k, sub, 1 - c)
            i = t["sib" + name][e]
            rcopy(ref, ref, i, i, g, b).wait_recv()

    run(
        "mid",
        {"o": d.Y, "v": d.Z},
        mid_axis,
        lambda name, off, sub: mid_block(name, off),
        1,
        None,
    )
    run(
        "last",
        {"o": d.Z, "v": d.Y},
        last_axis,
        lambda name, off, sub: last_block(name, off, sub, c),
        nsub,
        sibling,
    )
    from_sibling("v")

    def tiles_of(ref, i):
        return ref[i // 2, lax.rem(i, 2)].reshape(d.K, TW, TW)

    @pl.loop(0, d.NT)
    def _(kk):
        j = lax.rem(b // d.HP + kk, d.NT)
        row = owner_ref[j]
        tiles = tiles_of(gv, row)
        left = jnp.concatenate([tiles[s] for s in range(d.K)], axis=1)
        right = jnp.concatenate(
            [bm[lax.rem(row + voff_ref[s], d.NT)] for s in range(d.K)], axis=0
        )
        value = jnp.dot(left, right, preferred_element_type=F32).astype(BF16)
        for h in range(d.HP):
            to = j * d.HP + h
            rbuf[to] = value[h * d.CH : (h + 1) * d.CH]

            @pl.when(to != b)
            def _():
                rcopy(rbuf.at[to], rb.at[b], t["R"] + to, t["R"] + b, g, to).start()

            @pl.when(to == b)
            def _():
                rb[b] = value[h * d.CH : (h + 1) * d.CH]

    from_sibling("o")

    @pl.loop(0, d.NT)
    def _(kk):
        j = lax.rem(g + kk, d.NT)
        col = owner_ref[j]
        lefts, rights = [], []
        for s in range(d.K):
            i = lax.rem(col - ooff_ref[s] + d.NT, d.NT)
            lefts.append(bt[i])
            per = d.NB // d.K
            rows = go[i // 2, lax.rem(i, 2)].reshape(d.K, TW, TW)[s]
            rights.append(rows)
        value = jnp.dot(
            jnp.concatenate(lefts, axis=1),
            jnp.concatenate(rights, axis=0),
            preferred_element_type=F32,
        ).astype(BF16)
        lbuf[j] = value

        @pl.when(j != g)
        def _():
            rcopy(lbuf.at[j], lg.at[g], t["Lg"] + j, t["Lg"] + g, j, b).start()

        @pl.when(j == g)
        def _():
            lg[g] = value

    @pl.loop(0, d.NT)
    def _(kk):
        j = lax.rem(g - kk + d.NT, d.NT)

        @pl.when(j != g)
        def _():
            rcopy(lg.at[j], lg.at[j], t["Lg"] + j, t["Lg"] + j, j, b).wait_recv()

        for h in range(d.HP):
            to = j * d.HP + h
            src = lg.at[j, pl.ds(h * d.CH, d.CH)]

            @pl.when(to != b)
            def _():
                rcopy(src, lb.at[b], t["Lb"] + to, t["Lb"] + b, g, to).start()

            @pl.when(to == b)
            def _():
                lb[b] = src[...]

    @pl.loop(1, d.NB)
    def _(k):
        q = lax.rem(b + k, d.NB)
        rcopy(rb.at[q], rb.at[q], t["R"] + q, t["R"] + q, g, q).wait_recv()

    @pl.loop(1, d.NB)
    def _(k):
        q = lax.rem(b + k, d.NB)
        rcopy(lb.at[q], lb.at[q], t["Lb"] + q, t["Lb"] + q, g, q).wait_recv()

    n16 = d.NB * 16
    prod = jnp.zeros((n16, n16), F32)
    for r in range(d.CH // 16):
        left = lb[:, 16 * r : 16 * r + 16, :].reshape(n16, TW)
        right = rb[:, 16 * r : 16 * r + 16, :].reshape(n16, TW)
        prod = prod + lax.dot_general(
            left, right, (((1,), (1,)), ((), ())), preferred_element_type=F32
        )
    ii = lax.broadcasted_iota(jnp.int32, (n16, n16), 0)
    jj = lax.broadcasted_iota(jnp.int32, (n16, n16), 1)
    prod = jnp.where((ii & 15) == (jj & 15), prod, 0.0)
    folded = jnp.sum(prod.reshape(d.NB, 16, n16), axis=1)
    pick = (
        lax.broadcasted_iota(jnp.int32, (n16, TW), 0) // 16
        == lax.broadcasted_iota(jnp.int32, (n16, TW), 1)
    ).astype(F32)
    part = jnp.dot(
        folded, pick, precision=lax.Precision.HIGHEST, preferred_element_type=F32
    )
    s1[...] = jnp.broadcast_to(part[:, None, :], (d.NB, 8, TW))
    s1r[b] = s1[b]

    @pl.loop(1, d.NB)
    def _(k):
        q = lax.rem(b + k, d.NB)
        rcopy(s1.at[q], s1r.at[b], t["S1"] + q, t["S1"] + b, g, q).start()

    @pl.loop(1, d.NB)
    def _(k):
        q = lax.rem(b + k, d.NB)
        rcopy(s1r.at[q], s1r.at[q], t["S1"] + q, t["S1"] + q, g, q).wait_recv()

    s2[g] = jnp.sum(s1r[...], axis=0)

    @pl.loop(1, d.NG)
    def _(k):
        q = lax.rem(g + k, d.NG)
        rcopy(s2.at[g], s2.at[g], t["S2"] + q, t["S2"] + g, q, b).start()

    @pl.loop(1, d.NG)
    def _(k):
        q = lax.rem(g + k, d.NG)
        rcopy(s2.at[q], s2.at[q], t["S2"] + q, t["S2"] + q, q, b).wait_recv()

    total = jnp.sum(s2[...], axis=0)
    out_ref[...] = total[0:1, : d.NB] * (1.0 / (d.NT * TW))

    for cp in sends:
        cp.wait_send()

    @pl.loop(1, d.NB)
    def _(k):
        q = lax.rem(b + k, d.NB)
        rcopy(rbuf.at[q], rbuf.at[q], t["R"] + q, t["R"] + q, g, q).wait_send()
        rcopy(rbuf.at[q], rbuf.at[q], t["Lb"] + q, t["Lb"] + q, g, q).wait_send()
        rcopy(s1.at[q], s1.at[q], t["S1"] + q, t["S1"] + q, g, q).wait_send()

    @pl.loop(1, d.NG)
    def _(k):
        q = lax.rem(g + k, d.NG)
        rcopy(lbuf.at[q], lbuf.at[q], t["Lg"] + q, t["Lg"] + q, q, b).wait_send()
        rcopy(s2.at[q], s2.at[q], t["S2"] + q, t["S2"] + q, q, b).wait_send()


def make(d, nsub):
    t, nsem = layout(d, nsub)

    def body(integrals, mask, owner, otiles, ooff, vtiles, voff):
        vmem = pl.BlockSpec(memory_space=pltpu.VMEM)
        smem = pl.BlockSpec(memory_space=pltpu.SMEM)
        gshape = (d.Z, 2, d.Y, d.X, d.RPD, TW)
        return pl.pallas_call(
            functools.partial(kernel, d, nsub, t),
            out_shape=jax.ShapeDtypeStruct((1, d.NB), F32),
            in_specs=[smem] * 4 + [vmem] * 3,
            out_specs=vmem,
            scratch_shapes=[
                pltpu.VMEM(gshape, BF16),
                pltpu.VMEM(gshape, BF16),
                pltpu.VMEM((d.NT, TW, TW), BF16),
                pltpu.VMEM((d.NT, TW, TW), BF16),
                pltpu.VMEM((d.NB, d.CH, TW), BF16),
                pltpu.VMEM((d.NB, d.CH, TW), BF16),
                pltpu.VMEM((d.NT, TW, TW), BF16),
                pltpu.VMEM((d.NT, TW, TW), BF16),
                pltpu.VMEM((d.NB, d.CH, TW), BF16),
                pltpu.VMEM((d.NB, 8, TW), F32),
                pltpu.VMEM((d.NB, 8, TW), F32),
                pltpu.VMEM((d.NG, 8, TW), F32),
                pltpu.SemaphoreType.DMA((nsem,)),
                pltpu.SemaphoreType.DMA((nsem,)),
            ],
            compiler_params=pltpu.CompilerParams(
                collective_id=0, has_side_effects=True, vmem_limit_bytes=40 << 20
            ),
        )(mask, owner, ooff, voff, integrals, otiles, vtiles)

    return body


def solution(mesh, x=4, kcount=8, nsub=2):
    d = Dims(mesh.shape["grp"], mesh.shape["blk"], x, kcount)
    in_specs = (
        P("blk", None, "grp"),
        P(),
        P(),
        P(("grp", "blk"), None),
        P(),
        P(("grp", "blk"), None),
        P(),
    )
    return jax.shard_map(
        make(d, nsub), mesh=mesh, in_specs=in_specs, out_specs=P("blk", None), check_vma=False
    )
```

time: 428 us -> 117 us (0.27)
  waiting for transfers between devices: 207 us -> 0 us
  Pallas kernels: 0 us -> 111 us
  blocking collectives: 98.2 us -> 0 us
  local copies, waits for them, and re-layouts: 66.5 us -> 5.61 us
  starting transfers between devices: 18.1 us -> 0 us
  between operations: 13.9 us -> 0.02 us
  matrix products: 12.2 us -> 0 us
  other arithmetic: 10.9 us -> 0 us
    all_gather x2 -> x0, waiting for transfers between devices: 184 us -> none  [the longest x1 102 us: body(): lax.all_gather(occupied_tiles, ('grp', 'blk'), axis=0, tiled=True)]
    pallas_call x0 -> x1, Pallas kernels: none -> 111 us  [body(): pl.pallas_call(functools.partial(kernel, d, nsub, t), out_shape=jax.Shape...]
    psum x1 -> x0, blocking collectives: 98.2 us -> none  [body(): total = lax.psum(partial_sum, ('grp', 'blk'))]
    gather x25 -> x0, local copies, waits for them, and re-layouts: 52.3 us -> none  [the longest x8 25.8 us: body(): occupied_pick = occupied_all[source_rows[:, slot], slot]]
    all_to_all x3 -> x0, waiting for transfers between devices: 22.1 us -> none  [the longest x1 11.3 us: body(): lax.all_to_all(occupied_moved, 'blk', split_axis=2, concat_axis=0, tiled=...]
    all_to_all x3 -> x0, starting transfers between devices: 18.1 us -> none  [the longest x1 6.86 us: body(): lax.all_to_all(virtual_part, 'blk', split_axis=2, concat_axis=0, tiled=True)]
    dot_general x17 -> x0, matrix products: 12.2 us -> none  [the longest x8 6.22 us: body(): jnp.einsum('tmn,ptml->ptnl', occupied_pick, occupied_inputs, preferred_el...]
    unnamed x2 -> x0, other arithmetic: 7.41 us -> none
  transfers between devices with their start and end apart: 5 -> 0, of which waited for: 4 -> 0; matrix products, arithmetic and copies ran while one was open for 20% -> 0% of each run, Pallas kernels for 0% -> 0%
where the time goes in v1:
time: 117 us; the launch traced here: 116 us
  Pallas kernels  111 us (95%)
  local copies, waits for them, and re-layouts  5.61 us (5%)
    pallas_call x1, Pallas kernels, body(): pl.pallas_call(functools.partial(kernel, d, nsub, t), out_shape=jax.Shape...  111 us
    unnamed x15, local copies, waits for them, and re-layouts  5.61 us

profile of v1, /device:TPU:1, one launch (start us, length us, event | category | flops | bytes accessed | tf_op | source)
XLA Modules:
  0.0 116.4 jit_solution(12898948429754603534)
XLA Ops:
  0.0 0.0 copy-start
  0.0 1.0 copy-done
  1.0 0.0 copy-start.1
  1.0 0.7 copy-done.1
  1.7 0.0 copy-start.2
  1.7 0.7 copy-done.2
  2.4 0.0 copy-start.3
  2.4 0.7 copy-done.3
  3.1 0.0 copy-start.4
  3.1 0.7 copy-done.4
  3.8 0.0 copy-start.5
  3.8 0.7 copy-done.5
  4.4 0.0 copy-start.6
  4.4 0.7 copy-done.6
  5.1 110.8 %shard_map.73 = f32[1,32]{1,0:T(1,128)S(1)} custom-call(s32[16,16]{1,0:T(8,128)S(1)} %copy-done.1, s32[16]{0:T(128)S(1)} %copy-done.4, s32[8]{0:T(128)S(1)} %copy-done.5, s32[8]{0:T(128)S(1)} %copy-done.6, bf16[1,2048,128]{2,1,0:T(8,128)(2,1)S(1)} %copy-done, bf16[32,128]{1,0:T(8,128)(2,1)S(1)} %copy-done.2, bf16[32,128]{1,0:T(8,128)(2,1)S(1)} %copy-done.3), custom_call_target="tpu_custom_call" | custom-call | tf_op jit(solution)/shard_map/pallas_call | solution.py:412
  115.9 0.5 copy.9
Async XLA Ops:
  0.0 1.0 copy-start
  1.0 0.7 copy-start.1
  1.7 0.7 copy-start.2
  2.4 0.7 copy-start.3
  3.1 0.7 copy-start.4
  3.8 0.7 copy-start.5
  4.4 0.7 copy-start.6

commit v2 on v1

--- a/solution.py
+++ b/solution.py
@@ -49,12 +49,8 @@
 def layout(d, nsub):
     s = Sems()
     t = {}
-    for name in ("o", "v"):
-        t["x" + name] = s.take(d.X)
-    mid = {"o": d.Y, "v": d.Z}
     last = {"o": d.Z, "v": d.Y}
     for name in ("o", "v"):
-        t["mid" + name] = {e: s.take() for e in ring_plan(mid[name], 1)}
         t["last" + name] = {e: s.take() for e in ring_plan(last[name], nsub)}
         t["sib" + name] = {e: s.take() for e in ring_plan(last[name], nsub)}
         t["own" + name] = s.take()
@@ -63,6 +59,9 @@
     t["Lb"] = s.take(d.NB)
     t["S1"] = s.take(d.NB)
     t["S2"] = s.take(d.NG)
+    t["Po"] = s.take(d.Y * d.X)
+    t["Pv"] = s.take(d.Z * d.X)
+    t["in"] = s.take(7)
     return t, s.count
 
 
@@ -70,14 +69,19 @@
     d,
     nsub,
     t,
+    mask_hbm,
+    owner_hbm,
+    ooff_hbm,
+    voff_hbm,
+    b_hbm,
+    ot_ref,
+    vt_ref,
+    out_ref,
     mask_ref,
     owner_ref,
     ooff_ref,
     voff_ref,
     b_ref,
-    ot_ref,
-    vt_ref,
-    out_ref,
     go,
     gv,
     bm,
@@ -111,32 +115,67 @@
 
     barrier = pltpu.get_barrier_semaphore()
 
+    def signal(gg, bb):
+        pl.semaphore_signal(barrier, inc=1, device_id=(gg, bb), device_id_type=MESH)
+
     @pl.loop(1, d.NG)
     def _(k):
-        pl.semaphore_signal(
-            barrier, inc=1, device_id=(lax.rem(g + k, d.NG), b), device_id_type=MESH
+        signal(lax.rem(g + k, d.NG), b)
+
+    @pl.loop(1, d.NB)
+    def _(k):
+        signal(g, lax.rem(b + k, d.NB))
+
+    for dx in range(1, d.X):
+
+        @pl.loop(1, d.Z)
+        def _(k):
+            signal(lax.rem(z + k, d.Z) * 2 + c, y * d.X + lax.rem(x + dx, d.X))
+
+    loads = [
+        pltpu.make_async_copy(src, dst, ssem.at[t["in"] + i])
+        for i, (src, dst) in enumerate(
+            [
+                (ot_ref, go.at[z, c, y, x]),
+                (vt_ref, gv.at[z, c, y, x]),
+                (mask_hbm, mask_ref),
+                (owner_hbm, owner_ref),
+                (ooff_hbm, ooff_ref),
+                (voff_hbm, voff_ref),
+                (b_hbm, b_ref),
+            ]
         )
-
-    @pl.loop(1, d.NB)
-    def _(k):
-        pl.semaphore_signal(
-            barrier, inc=1, device_id=(g, lax.rem(b + k, d.NB)), device_id_type=MESH
-        )
-
-    go[z, c, y, x] = ot_ref[...]
-    gv[z, c, y, x] = vt_ref[...]
-    pl.semaphore_wait(barrier, d.NG + d.NB - 2)
-
-    bufs = {"o": go, "v": gv}
+    ]
+    for cp in loads:
+        cp.start()
+    pl.semaphore_wait(barrier, d.NG + d.NB - 2 + (d.X - 1) * (d.Z - 1))
+
     sends = []
 
-    for k in range(1, d.X):
-        for name in ("o", "v"):
-            ref = bufs[name].at[z, c, y, x]
-            i = t["x" + name] + k
-            cp = rcopy(ref, ref, i, i, g, y * d.X + lax.rem(x + k, d.X))
-            cp.start()
-            sends.append(cp)
+    def plane_copy(name, k, incoming):
+        sign = -1 if incoming else 1
+        dx = lax.rem(k, d.X)
+        xx = lax.rem(x + sign * dx + d.X, d.X)
+        if name == "o":
+            yy = lax.rem(y + sign * (k // d.X) + d.Y, d.Y)
+            dst = go.at[z, c, yy, xx] if incoming else go.at[z, c, y, x]
+            src, to = ot_ref, (g, yy * d.X + xx)
+        else:
+            zz = lax.rem(z + sign * (k // d.X) + d.Z, d.Z)
+            dst = gv.at[zz, c, y, xx] if incoming else gv.at[z, c, y, x]
+            src, to = vt_ref, (zz * 2 + c, y * d.X + xx)
+        i = t["P" + name] + k
+        return rcopy(dst if incoming else src, dst, i, i, *to)
+
+    plane = {"o": d.Y * d.X, "v": d.Z * d.X}
+    for name in ("o", "v"):
+
+        @pl.loop(1, plane[name])
+        def _(k):
+            plane_copy(name, k, False).start()
+
+    for cp in loads:
+        cp.wait()
 
     own = owner_ref[g]
 
@@ -147,11 +186,11 @@
         bm[i] = tile
         bt[i] = tile.T
 
-    for k in range(1, d.X):
-        for name in ("o", "v"):
-            ref = bufs[name].at[z, c, y, lax.rem(x - k + d.X, d.X)]
-            i = t["x" + name] + k
-            rcopy(ref, ref, i, i, g, b).wait_recv()
+    for name in ("o", "v"):
+
+        @pl.loop(1, plane[name])
+        def _(k):
+            plane_copy(name, k, True).wait_recv()
 
     def along_z(k):
         return lax.rem(z + k + d.Z, d.Z) * 2 + c, b
@@ -164,11 +203,6 @@
 
     def pos_y(k):
         return lax.rem(y + k + d.Y, d.Y)
-
-    def mid_block(name, off):
-        if name == "o":
-            return go.at[z, c, pos_y(off)]
-        return gv.at[pos_z(off), c, y]
 
     def last_block(name, off, sub, core):
         if name == "o":
@@ -177,7 +211,6 @@
         h = d.Z // nsub
         return gv.at[pl.ds(sub * h, h), core, pos_y(off)]
 
-    mid_axis = {"o": along_y, "v": along_z}
     last_axis = {"o": along_z, "v": along_y}
 
     def run(stage, sizes, axis, block, nsubs, forward):
@@ -238,14 +271,6 @@
             rcopy(ref, ref, i, i, g, b).wait_recv()
 
     run(
-        "mid",
-        {"o": d.Y, "v": d.Z},
-        mid_axis,
-        lambda name, off, sub: mid_block(name, off),
-        1,
-        None,
-    )
-    run(
         "last",
         {"o": d.Z, "v": d.Y},
         last_axis,
@@ -258,7 +283,7 @@
     def tiles_of(ref, i):
         return ref[i // 2, lax.rem(i, 2)].reshape(d.K, TW, TW)
 
-    @pl.loop(0, d.NT)
+    @pl.loop(0, d.NT, unroll=2)
     def _(kk):
         j = lax.rem(b // d.HP + kk, d.NT)
         row = owner_ref[j]
@@ -282,15 +307,14 @@
 
     from_sibling("o")
 
-    @pl.loop(0, d.NT)
+    @pl.loop(0, d.NT, unroll=2)
     def _(kk):
-        j = lax.rem(g + kk, d.NT)
+        j = lax.rem(g + kk + b // d.HP, d.NT)
         col = owner_ref[j]
         lefts, rights = [], []
         for s in range(d.K):
             i = lax.rem(col - ooff_ref[s] + d.NT, d.NT)
             lefts.append(bt[i])
-            per = d.NB // d.K
             rows = go[i // 2, lax.rem(i, 2)].reshape(d.K, TW, TW)[s]
             rights.append(rows)
         value = jnp.dot(
@@ -310,7 +334,7 @@
 
     @pl.loop(0, d.NT)
     def _(kk):
-        j = lax.rem(g - kk + d.NT, d.NT)
+        j = lax.rem(g - kk - b // d.HP + 2 * d.NT, d.NT)
 
         @pl.when(j != g)
         def _():
@@ -328,15 +352,29 @@
             def _():
                 lb[b] = src[...]
 
+    for name in ("o", "v"):
+
+        @pl.loop(1, plane[name])
+        def _(k):
+            plane_copy(name, k, False).wait_send()
+
+    for cp in sends:
+        cp.wait_send()
+
     @pl.loop(1, d.NB)
     def _(k):
         q = lax.rem(b + k, d.NB)
-        rcopy(rb.at[q], rb.at[q], t["R"] + q, t["R"] + q, g, q).wait_recv()
+        rcopy(rb.at[q], rb.at[q], t["R"] + q, t["R"] + q, g, q).wait()
+
+    @pl.loop(1, d.NG)
+    def _(k):
+        q = lax.rem(g + k, d.NG)
+        rcopy(lbuf.at[q], lbuf.at[q], t["Lg"] + q, t["Lg"] + q, q, b).wait_send()
 
     @pl.loop(1, d.NB)
     def _(k):
         q = lax.rem(b + k, d.NB)
-        rcopy(lb.at[q], lb.at[q], t["Lb"] + q, t["Lb"] + q, g, q).wait_recv()
+        rcopy(lb.at[q], lb.at[q], t["Lb"] + q, t["Lb"] + q, g, q).wait()
 
     n16 = d.NB * 16
     prod = jnp.zeros((n16, n16), F32)
@@ -357,7 +395,8 @@
     part = jnp.dot(
         folded, pick, precision=lax.Precision.HIGHEST, preferred_element_type=F32
     )
-    s1[...] = jnp.broadcast_to(part[:, None, :], (d.NB, 8, TW))
+    for p in range(d.NB):
+        s1[p] = part[p : p + 1]
     s1r[b] = s1[b]
 
     @pl.loop(1, d.NB)
@@ -377,29 +416,18 @@
         q = lax.rem(g + k, d.NG)
         rcopy(s2.at[g], s2.at[g], t["S2"] + q, t["S2"] + g, q, b).start()
 
+    @pl.loop(1, d.NB)
+    def _(k):
+        q = lax.rem(b + k, d.NB)
+        rcopy(s1.at[q], s1.at[q], t["S1"] + q, t["S1"] + q, g, q).wait_send()
+
     @pl.loop(1, d.NG)
     def _(k):
         q = lax.rem(g + k, d.NG)
-        rcopy(s2.at[q], s2.at[q], t["S2"] + q, t["S2"] + q, q, b).wait_recv()
+        rcopy(s2.at[q], s2.at[q], t["S2"] + q, t["S2"] + q, q, b).wait()
 
     total = jnp.sum(s2[...], axis=0)
-    out_ref[...] = total[0:1, : d.NB] * (1.0 / (d.NT * TW))
-
-    for cp in sends:
-        cp.wait_send()
-
-    @pl.loop(1, d.NB)
-    def _(k):
-        q = lax.rem(b + k, d.NB)
-        rcopy(rbuf.at[q], rbuf.at[q], t["R"] + q, t["R"] + q, g, q).wait_send()
-        rcopy(rbuf.at[q], rbuf.at[q], t["Lb"] + q, t["Lb"] + q, g, q).wait_send()
-        rcopy(s1.at[q], s1.at[q], t["S1"] + q, t["S1"] + q, g, q).wait_send()
-
-    @pl.loop(1, d.NG)
-    def _(k):
-        q = lax.rem(g + k, d.NG)
-        rcopy(lbuf.at[q], lbuf.at[q], t["Lg"] + q, t["Lg"] + q, q, b).wait_send()
-        rcopy(s2.at[q], s2.at[q], t["S2"] + q, t["S2"] + q, q, b).wait_send()
+    out_ref[...] = total[:, : d.NB] * (1.0 / (d.NT * TW))
 
 
 def make(d, nsub):
@@ -407,14 +435,19 @@
 
     def body(integrals, mask, owner, otiles, ooff, vtiles, voff):
         vmem = pl.BlockSpec(memory_space=pltpu.VMEM)
-        smem = pl.BlockSpec(memory_space=pltpu.SMEM)
+        hbm = pl.BlockSpec(memory_space=pltpu.HBM)
         gshape = (d.Z, 2, d.Y, d.X, d.RPD, TW)
         return pl.pallas_call(
             functools.partial(kernel, d, nsub, t),
             out_shape=jax.ShapeDtypeStruct((1, d.NB), F32),
-            in_specs=[smem] * 4 + [vmem] * 3,
+            in_specs=[hbm] * 7,
             out_specs=vmem,
             scratch_shapes=[
+                pltpu.SMEM((d.NT, d.NT), jnp.int32),
+                pltpu.SMEM((d.NT,), jnp.int32),
+                pltpu.SMEM((d.K,), jnp.int32),
+                pltpu.SMEM((d.K,), jnp.int32),
+                pltpu.VMEM((1, d.NT * TW, TW), BF16),
                 pltpu.VMEM(gshape, BF16),
                 pltpu.VMEM(gshape, BF16),
                 pltpu.VMEM((d.NT, TW, TW), BF16),
@@ -424,14 +457,14 @@
                 pltpu.VMEM((d.NT, TW, TW), BF16),
                 pltpu.VMEM((d.NT, TW, TW), BF16),
                 pltpu.VMEM((d.NB, d.CH, TW), BF16),
-                pltpu.VMEM((d.NB, 8, TW), F32),
-                pltpu.VMEM((d.NB, 8, TW), F32),
-                pltpu.VMEM((d.NG, 8, TW), F32),
+                pltpu.VMEM((d.NB, 1, TW), F32),
+                pltpu.VMEM((d.NB, 1, TW), F32),
+                pltpu.VMEM((d.NG, 1, TW), F32),
                 pltpu.SemaphoreType.DMA((nsem,)),
                 pltpu.SemaphoreType.DMA((nsem,)),
             ],
             compiler_params=pltpu.CompilerParams(
-                collective_id=0, has_side_effects=True, vmem_limit_bytes=40 << 20
+                collective_id=0, has_side_effects=True, vmem_limit_bytes=60 << 20
             ),
         )(mask, owner, ooff, voff, integrals, otiles, vtiles)
 

time: 117 us -> 103 us (0.88)
  Pallas kernels: 111 us -> 102 us
  local copies, waits for them, and re-layouts: 5.61 us -> 1.19 us
    pallas_call x1, Pallas kernels: 111 us -> 102 us  [body(): pl.pallas_call(functools.partial(kernel, d, nsub, t), out_shape=jax.Shape...]
    unnamed x15 -> x1, local copies, waits for them, and re-layouts: 5.61 us -> 1.19 us
where the time goes in v2:
time: 103 us
  Pallas kernels  102 us (99%)
  local copies, waits for them, and re-layouts  1.19 us (1%)
    pallas_call x1, Pallas kernels, body(): pl.pallas_call(functools.partial(kernel, d, nsub, t), out_shape=jax.Shape...  102 us

profile of v2, /device:TPU:1, one launch (start us, length us, event | category | flops | bytes accessed | tf_op | source)
XLA Modules:
  0.0 103.1 jit_solution(18437642427144947388)
XLA Ops:
  0.0 101.9 %shard_map.73 = f32[1,32]{1,0:T(1,128)} custom-call(s32[16,16]{1,0:T(8,128)} %mask_hbm.1, s32[16]{0:T(128)} %owner_hbm.1, s32[8]{0:T(128)} %ooff_hbm.1, s32[8]{0:T(128)} %voff_hbm.1, bf16[1,2048,128]{2,1,0:T(8,128)(2,1)} %b_hbm.1, bf16[32,128]{1,0:T(8,128)(2,1)} %ot_ref.1, bf16[32,128]{1,0:T(8,128)(2,1)} %vt_ref.1), custom_call_target="tpu_custom_call" | custom-call | tf_op jit(solution)/shard_map/pallas_call | solution.py:440
  101.9 1.2 %copy.9 = f32[1,32]{1,0:T(1,128)} copy(f32[1,32]{1,0:T(1,128)} %shard_map.73) | data formatting | bytes 256

commit v3 on v2

--- a/solution.py
+++ b/solution.py
@@ -8,6 +8,7 @@
 from jax.sharding import PartitionSpec as P
 
 MESH = pl.DeviceIdType.MESH
+SCHEDULE = (("L", 0, 16), ("R", 0, 16))
 TW = 128
 F32 = jnp.float32
 BF16 = jnp.bfloat16
@@ -52,15 +53,10 @@
     last = {"o": d.Z, "v": d.Y}
     for name in ("o", "v"):
         t["last" + name] = {e: s.take() for e in ring_plan(last[name], nsub)}
-        t["sib" + name] = {e: s.take() for e in ring_plan(last[name], nsub)}
-        t["own" + name] = s.take()
-    t["R"] = s.take(d.NB)
-    t["Lg"] = s.take(d.NG)
-    t["Lb"] = s.take(d.NB)
-    t["S1"] = s.take(d.NB)
-    t["S2"] = s.take(d.NG)
-    t["Po"] = s.take(d.Y * d.X)
-    t["Pv"] = s.take(d.Z * d.X)
+        for stage in ("P", "ring", "sib"):
+            t[stage + name] = s.take()
+    for name in ("R", "Lb", "S1", "S2"):
+        t[name] = s.take()
     t["in"] = s.take(7)
     return t, s.count
 
@@ -89,7 +85,6 @@
     rbuf,
     rb,
     lbuf,
-    lg,
     lb,
     s1,
     s1r,
@@ -113,31 +108,10 @@
             device_id_type=MESH,
         )
 
-    barrier = pltpu.get_barrier_semaphore()
-
-    def signal(gg, bb):
-        pl.semaphore_signal(barrier, inc=1, device_id=(gg, bb), device_id_type=MESH)
-
-    @pl.loop(1, d.NG)
-    def _(k):
-        signal(lax.rem(g + k, d.NG), b)
-
-    @pl.loop(1, d.NB)
-    def _(k):
-        signal(g, lax.rem(b + k, d.NB))
-
-    for dx in range(1, d.X):
-
-        @pl.loop(1, d.Z)
-        def _(k):
-            signal(lax.rem(z + k, d.Z) * 2 + c, y * d.X + lax.rem(x + dx, d.X))
-
     loads = [
         pltpu.make_async_copy(src, dst, ssem.at[t["in"] + i])
         for i, (src, dst) in enumerate(
             [
-                (ot_ref, go.at[z, c, y, x]),
-                (vt_ref, gv.at[z, c, y, x]),
                 (mask_hbm, mask_ref),
                 (owner_hbm, owner_ref),
                 (ooff_hbm, ooff_ref),
@@ -148,31 +122,64 @@
     ]
     for cp in loads:
         cp.start()
-    pl.semaphore_wait(barrier, d.NG + d.NB - 2 + (d.X - 1) * (d.Z - 1))
-
-    sends = []
-
-    def plane_copy(name, k, incoming):
-        sign = -1 if incoming else 1
-        dx = lax.rem(k, d.X)
-        xx = lax.rem(x + sign * dx + d.X, d.X)
+    pltpu.make_async_copy(ot_ref, go.at[z, c, y, x], rsem.at[t["Po"]]).start()
+    pltpu.make_async_copy(vt_ref, gv.at[z, c, y, x], rsem.at[t["Pv"]]).start()
+
+    barrier = pltpu.get_barrier_semaphore()
+
+    def signal(gg, bb):
+        pl.semaphore_signal(barrier, inc=1, device_id=(gg, bb), device_id_type=MESH)
+
+    @pl.loop(1, d.NG)
+    def _(k):
+        signal(lax.rem(g + k, d.NG), b)
+
+    @pl.loop(1, d.NB)
+    def _(k):
+        signal(g, lax.rem(b + k, d.NB))
+
+    for dx in range(1, d.X):
+
+        @pl.loop(1, d.Z)
+        def _(k):
+            signal(lax.rem(z + k, d.Z) * 2 + c, y * d.X + lax.rem(x + dx, d.X))
+
+    source = lax.rem((g + d.NG - b // d.HP) * 7, d.NG)
+
+    @pl.loop(0, d.NB)
+    def _(k):
+        @pl.when((source != g) | (k != b))
+        def _():
+            signal(source, k)
+
+    others = d.NG + d.NB - 2 + (d.X - 1) * (d.Z - 1) + d.NB
+    pl.semaphore_wait(barrier, others - (source == g).astype(jnp.int32))
+
+    bufs = {"o": go, "v": gv}
+
+    def plane_copy(name, k):
+        xx = lax.rem(x + lax.rem(k, d.X), d.X)
         if name == "o":
-            yy = lax.rem(y + sign * (k // d.X) + d.Y, d.Y)
-            dst = go.at[z, c, yy, xx] if incoming else go.at[z, c, y, x]
-            src, to = ot_ref, (g, yy * d.X + xx)
+            ref, src = go.at[z, c, y, x], ot_ref
+            to = (g, lax.rem(y + k // d.X, d.Y) * d.X + xx)
         else:
-            zz = lax.rem(z + sign * (k // d.X) + d.Z, d.Z)
-            dst = gv.at[zz, c, y, xx] if incoming else gv.at[z, c, y, x]
-            src, to = vt_ref, (zz * 2 + c, y * d.X + xx)
-        i = t["P" + name] + k
-        return rcopy(dst if incoming else src, dst, i, i, *to)
+            ref, src = gv.at[z, c, y, x], vt_ref
+            to = (lax.rem(z + k // d.X, d.Z) * 2 + c, y * d.X + xx)
+        i = t["P" + name]
+        return rcopy(src, ref, i, i, *to)
+
+    def plane_bytes(name):
+        n = plane[name] - 1
+        ref = rbuf.reshape(d.NB * d.CH, TW).at[pl.ds(0, n * d.RPD)]
+        i = t["P" + name]
+        return rcopy(ref, ref, i, i, g, b)
 
     plane = {"o": d.Y * d.X, "v": d.Z * d.X}
     for name in ("o", "v"):
 
         @pl.loop(1, plane[name])
         def _(k):
-            plane_copy(name, k, False).start()
+            plane_copy(name, k).start()
 
     for cp in loads:
         cp.wait()
@@ -187,10 +194,8 @@
         bt[i] = tile.T
 
     for name in ("o", "v"):
-
-        @pl.loop(1, plane[name])
-        def _(k):
-            plane_copy(name, k, True).wait_recv()
+        ref = go.at[z, c] if name == "o" else gv.at[:, c, y]
+        rcopy(ref, ref, t["P" + name], t["P" + name], g, b).wait_recv()
 
     def along_z(k):
         return lax.rem(z + k + d.Z, d.Z) * 2 + c, b
@@ -219,10 +224,7 @@
         def send(name, e):
             dirn, k, sub = e
             ref = block(name, -dirn * (k - 1), sub)
-            i = t[stage + name][e]
-            cp = rcopy(ref, ref, i, i, *axis[name](dirn))
-            cp.start()
-            sends.append(cp)
+            rcopy(ref, ref, t["ring" + name], t[stage + name][e], *axis[name](dirn)).start()
 
         for name in ("o", "v"):
             for e in plans[name]:
@@ -250,25 +252,16 @@
     def sibling(name, e):
         if e is None:
             ref = go.at[z, c] if name == "o" else gv.at[:, c, y]
-            i = t["own" + name]
         else:
             dirn, k, sub = e
             ref = last_block(name, -dirn * k, sub, c)
-            i = t["sib" + name][e]
-        cp = rcopy(ref, ref, i, i, sib, b)
-        cp.start()
-        sends.append(cp)
+        i = t["sib" + name]
+        rcopy(ref, ref, i, i, sib, b).start()
 
     def from_sibling(name):
-        ref = go.at[z, 1 - c] if name == "o" else gv.at[:, 1 - c, y]
-        i = t["own" + name]
+        ref = bufs[name].at[:, 1 - c]
+        i = t["sib" + name]
         rcopy(ref, ref, i, i, g, b).wait_recv()
-        n = d.Z if name == "o" else d.Y
-        for e in ring_plan(n, nsub):
-            dirn, k, sub = e
-            ref = last_block(name, -dirn * k, sub, 1 - c)
-            i = t["sib" + name][e]
-            rcopy(ref, ref, i, i, g, b).wait_recv()
 
     run(
         "last",
@@ -279,13 +272,14 @@
         sibling,
     )
     from_sibling("v")
+    from_sibling("o")
 
     def tiles_of(ref, i):
         return ref[i // 2, lax.rem(i, 2)].reshape(d.K, TW, TW)
 
-    @pl.loop(0, d.NT, unroll=2)
-    def _(kk):
-        j = lax.rem(b // d.HP + kk, d.NT)
+    def virtual_slot(kk):
+        at = lax.rem(b // d.HP + kk, d.NT)
+        j = lax.rem((g + d.NG - at) * 7, d.NG)
         row = owner_ref[j]
         tiles = tiles_of(gv, row)
         left = jnp.concatenate([tiles[s] for s in range(d.K)], axis=1)
@@ -294,22 +288,20 @@
         )
         value = jnp.dot(left, right, preferred_element_type=F32).astype(BF16)
         for h in range(d.HP):
-            to = j * d.HP + h
+            to = at * d.HP + h
             rbuf[to] = value[h * d.CH : (h + 1) * d.CH]
 
             @pl.when(to != b)
             def _():
-                rcopy(rbuf.at[to], rb.at[b], t["R"] + to, t["R"] + b, g, to).start()
+                rcopy(rbuf.at[to], rb.at[b], t["R"], t["R"], g, to).start()
 
             @pl.when(to == b)
             def _():
                 rb[b] = value[h * d.CH : (h + 1) * d.CH]
 
-    from_sibling("o")
-
-    @pl.loop(0, d.NT, unroll=2)
-    def _(kk):
-        j = lax.rem(g + kk + b // d.HP, d.NT)
+    def occupied_slot(kk):
+        at = lax.rem(b // d.HP + kk, d.NT)
+        j = lax.rem(at + 7 * g, d.NG)
         col = owner_ref[j]
         lefts, rights = [], []
         for s in range(d.K):
@@ -324,57 +316,47 @@
         ).astype(BF16)
         lbuf[j] = value
 
-        @pl.when(j != g)
-        def _():
-            rcopy(lbuf.at[j], lg.at[g], t["Lg"] + j, t["Lg"] + g, j, b).start()
-
-        @pl.when(j == g)
-        def _():
-            lg[g] = value
-
-    @pl.loop(0, d.NT)
-    def _(kk):
-        j = lax.rem(g - kk - b // d.HP + 2 * d.NT, d.NT)
-
-        @pl.when(j != g)
-        def _():
-            rcopy(lg.at[j], lg.at[j], t["Lg"] + j, t["Lg"] + j, j, b).wait_recv()
-
         for h in range(d.HP):
-            to = j * d.HP + h
-            src = lg.at[j, pl.ds(h * d.CH, d.CH)]
-
-            @pl.when(to != b)
+            to = at * d.HP + h
+            src = lbuf.at[j, pl.ds(h * d.CH, d.CH)]
+
+            @pl.when((to != b) | (j != g))
             def _():
-                rcopy(src, lb.at[b], t["Lb"] + to, t["Lb"] + b, g, to).start()
-
-            @pl.when(to == b)
+                rcopy(src, lb.at[b], t["Lb"], t["Lb"], j, to).start()
+
+            @pl.when((to == b) & (j == g))
             def _():
-                lb[b] = src[...]
+                lb[b] = value[h * d.CH : (h + 1) * d.CH]
+
+    steps = {"L": occupied_slot, "R": virtual_slot}
+    for what, lo, hi in SCHEDULE:
+
+        @pl.loop(lo * d.NT // 16, hi * d.NT // 16, unroll=2)
+        def _(kk):
+            steps[what](kk)
 
     for name in ("o", "v"):
-
-        @pl.loop(1, plane[name])
-        def _(k):
-            plane_copy(name, k, False).wait_send()
-
-    for cp in sends:
+        plane_bytes(name).wait_send()
+        ref = bufs[name].at[:, c]
+        rcopy(ref, ref, t["sib" + name], t["sib" + name], g, b).wait_send()
+        ref = bufs[name].at[pl.ds(0, d.Z - 1), c] if name == "o" else bufs[name].at[:, c, pl.ds(0, d.Y - 1)]
+        rcopy(ref, ref, t["ring" + name], t["ring" + name], g, b).wait_send()
+
+    def wait_all(ref, n, name):
+        part = ref.at[pl.ds(0, n)]
+        cp = rcopy(part, part, t[name], t[name], g, b)
         cp.wait_send()
-
-    @pl.loop(1, d.NB)
-    def _(k):
-        q = lax.rem(b + k, d.NB)
-        rcopy(rb.at[q], rb.at[q], t["R"] + q, t["R"] + q, g, q).wait()
-
-    @pl.loop(1, d.NG)
-    def _(k):
-        q = lax.rem(g + k, d.NG)
-        rcopy(lbuf.at[q], lbuf.at[q], t["Lg"] + q, t["Lg"] + q, q, b).wait_send()
-
-    @pl.loop(1, d.NB)
-    def _(k):
-        q = lax.rem(b + k, d.NB)
-        rcopy(lb.at[q], lb.at[q], t["Lb"] + q, t["Lb"] + q, g, q).wait()
+        cp.wait_recv()
+
+    wait_all(rb, d.NB - 1, "R")
+
+    @pl.when(source != g)
+    def _():
+        wait_all(lb, d.NB, "Lb")
+
+    @pl.when(source == g)
+    def _():
+        wait_all(lb, d.NB - 1, "Lb")
 
     n16 = d.NB * 16
     prod = jnp.zeros((n16, n16), F32)
@@ -402,30 +384,17 @@
     @pl.loop(1, d.NB)
     def _(k):
         q = lax.rem(b + k, d.NB)
-        rcopy(s1.at[q], s1r.at[b], t["S1"] + q, t["S1"] + b, g, q).start()
-
-    @pl.loop(1, d.NB)
-    def _(k):
-        q = lax.rem(b + k, d.NB)
-        rcopy(s1r.at[q], s1r.at[q], t["S1"] + q, t["S1"] + q, g, q).wait_recv()
-
+        rcopy(s1.at[q], s1r.at[b], t["S1"], t["S1"], g, q).start()
+
+    wait_all(s1r, d.NB - 1, "S1")
     s2[g] = jnp.sum(s1r[...], axis=0)
 
     @pl.loop(1, d.NG)
     def _(k):
         q = lax.rem(g + k, d.NG)
-        rcopy(s2.at[g], s2.at[g], t["S2"] + q, t["S2"] + g, q, b).start()
-
-    @pl.loop(1, d.NB)
-    def _(k):
-        q = lax.rem(b + k, d.NB)
-        rcopy(s1.at[q], s1.at[q], t["S1"] + q, t["S1"] + q, g, q).wait_send()
-
-    @pl.loop(1, d.NG)
-    def _(k):
-        q = lax.rem(g + k, d.NG)
-        rcopy(s2.at[q], s2.at[q], t["S2"] + q, t["S2"] + q, q, b).wait()
-
+        rcopy(s2.at[g], s2.at[g], t["S2"], t["S2"], q, b).start()
+
+    wait_all(s2, d.NG - 1, "S2")
     total = jnp.sum(s2[...], axis=0)
     out_ref[...] = total[:, : d.NB] * (1.0 / (d.NT * TW))
 
@@ -455,7 +424,6 @@
                 pltpu.VMEM((d.NB, d.CH, TW), BF16),
                 pltpu.VMEM((d.NB, d.CH, TW), BF16),
                 pltpu.VMEM((d.NT, TW, TW), BF16),
-                pltpu.VMEM((d.NT, TW, TW), BF16),
                 pltpu.VMEM((d.NB, d.CH, TW), BF16),
                 pltpu.VMEM((d.NB, 1, TW), F32),
                 pltpu.VMEM((d.NB, 1, TW), F32),

time: 103 us -> 95.5 us (0.927)
  Pallas kernels: 102 us -> 94.2 us
    pallas_call x1, Pallas kernels: 102 us -> 94.2 us  [body(): pl.pallas_call(functools.partial(kernel, d, nsub, t), out_shape=jax.Shape...]
where the time goes in v3:
time: 95.5 us; the launch traced here: 95.4 us
  Pallas kernels  94.2 us (99%)
  local copies, waits for them, and re-layouts  1.19 us (1%)
    pallas_call x1, Pallas kernels, body(): pl.pallas_call(functools.partial(kernel, d, nsub, t), out_shape=jax.Shape...  94.2 us

profile of v3, /device:TPU:1, one launch (start us, length us, event | category | flops | bytes accessed | tf_op | source)
XLA Modules:
  0.0 95.4 jit_solution(925405738954854805)
XLA Ops:
  0.0 94.2 %shard_map.73 = f32[1,32]{1,0:T(1,128)} custom-call(s32[16,16]{1,0:T(8,128)} %mask_hbm.1, s32[16]{0:T(128)} %owner_hbm.1, s32[8]{0:T(128)} %ooff_hbm.1, s32[8]{0:T(128)} %voff_hbm.1, bf16[1,2048,128]{2,1,0:T(8,128)(2,1)} %b_hbm.1, bf16[32,128]{1,0:T(8,128)(2,1)} %ot_ref.1, bf16[32,128]{1,0:T(8,128)(2,1)} %vt_ref.1), custom_call_target="tpu_custom_call" | custom-call | tf_op jit(solution)/shard_map/pallas_call | solution.py:409
  94.2 1.2 %copy.9 = f32[1,32]{1,0:T(1,128)} copy(f32[1,32]{1,0:T(1,128)} %shard_map.73) | data formatting | bytes 256

commit v4 on v3

--- a/solution.py
+++ b/solution.py
@@ -130,17 +130,17 @@
     def signal(gg, bb):
         pl.semaphore_signal(barrier, inc=1, device_id=(gg, bb), device_id_type=MESH)
 
-    @pl.loop(1, d.NG)
+    @pl.loop(1, d.NG, unroll=d.NG - 1)
     def _(k):
         signal(lax.rem(g + k, d.NG), b)
 
-    @pl.loop(1, d.NB)
+    @pl.loop(1, d.NB, unroll=d.NB - 1)
     def _(k):
         signal(g, lax.rem(b + k, d.NB))
 
     for dx in range(1, d.X):
 
-        @pl.loop(1, d.Z)
+        @pl.loop(1, d.Z, unroll=d.Z - 1)
         def _(k):
             signal(lax.rem(z + k, d.Z) * 2 + c, y * d.X + lax.rem(x + dx, d.X))
 
@@ -175,11 +175,18 @@
         return rcopy(ref, ref, i, i, g, b)
 
     plane = {"o": d.Y * d.X, "v": d.Z * d.X}
+
+    @pl.loop(1, min(plane.values()))
+    def _(k):
+        for name in ("o", "v"):
+            plane_copy(name, k).start()
+
     for name in ("o", "v"):
-
-        @pl.loop(1, plane[name])
-        def _(k):
-            plane_copy(name, k).start()
+        if plane[name] > min(plane.values()):
+
+            @pl.loop(min(plane.values()), plane[name])
+            def _(k):
+                plane_copy(name, k).start()
 
     for cp in loads:
         cp.wait()
@@ -193,7 +200,7 @@
         bm[i] = tile
         bt[i] = tile.T
 
-    for name in ("o", "v"):
+    def plane_arrived(name):
         ref = go.at[z, c] if name == "o" else gv.at[:, c, y]
         rcopy(ref, ref, t["P" + name], t["P" + name], g, b).wait_recv()
 
@@ -227,6 +234,7 @@
             rcopy(ref, ref, t["ring" + name], t[stage + name][e], *axis[name](dirn)).start()
 
         for name in ("o", "v"):
+            plane_arrived(name)
             for e in plans[name]:
                 if e[1] == 1:
                     send(name, e)
@@ -271,7 +279,6 @@
         nsub,
         sibling,
     )
-    from_sibling("v")
     from_sibling("o")
 
     def tiles_of(ref, i):
@@ -330,6 +337,8 @@
 
     steps = {"L": occupied_slot, "R": virtual_slot}
     for what, lo, hi in SCHEDULE:
+        if what == "R":
+            from_sibling("v")
 
         @pl.loop(lo * d.NT // 16, hi * d.NT // 16, unroll=2)
         def _(kk):
@@ -439,7 +448,7 @@
     return body
 
 
-def solution(mesh, x=4, kcount=8, nsub=2):
+def solution(mesh, x=4, kcount=8, nsub=4):
     d = Dims(mesh.shape["grp"], mesh.shape["blk"], x, kcount)
     in_specs = (
         P("blk", None, "grp"),

time: 95.5 us -> 94.3 us (0.987)
  Pallas kernels: 94.2 us -> 93 us
    pallas_call x1, Pallas kernels: 94.2 us -> 93 us  [body(): pl.pallas_call(functools.partial(kernel, d, nsub, t), out_shape=jax.Shape...]
where the time goes in v4:
time: 94.3 us; the launch traced here: 94.2 us
  Pallas kernels  93 us (99%)
  local copies, waits for them, and re-layouts  1.19 us (1%)
    pallas_call x1, Pallas kernels, body(): pl.pallas_call(functools.partial(kernel, d, nsub, t), out_shape=jax.Shape...  93 us

profile of v4, /device:TPU:1, one launch (start us, length us, event | category | flops | bytes accessed | tf_op | source)
XLA Modules:
  0.0 94.2 jit_solution(7771495425234408559)
XLA Ops:
  0.0 93.0 %shard_map.73 = f32[1,32]{1,0:T(1,128)} custom-call(s32[16,16]{1,0:T(8,128)} %mask_hbm.1, s32[16]{0:T(128)} %owner_hbm.1, s32[8]{0:T(128)} %ooff_hbm.1, s32[8]{0:T(128)} %voff_hbm.1, bf16[1,2048,128]{2,1,0:T(8,128)(2,1)} %b_hbm.1, bf16[32,128]{1,0:T(8,128)(2,1)} %ot_ref.1, bf16[32,128]{1,0:T(8,128)(2,1)} %vt_ref.1), custom_call_target="tpu_custom_call" | custom-call | tf_op jit(solution)/shard_map/pallas_call | solution.py:418
  93.0 1.2 %copy.9 = f32[1,32]{1,0:T(1,128)} copy(f32[1,32]{1,0:T(1,128)} %shard_map.73) | data formatting | bytes 256

commit v5 on v4

--- a/solution.py
+++ b/solution.py
@@ -158,6 +158,7 @@
     bufs = {"o": go, "v": gv}
 
     def plane_copy(name, k):
+        k = lax.rem(k + plane[name] // 2 - 1, plane[name] - 1) + 1
         xx = lax.rem(x + lax.rem(k, d.X), d.X)
         if name == "o":
             ref, src = go.at[z, c, y, x], ot_ref

time: 94.3 us -> 94.1 us (level)
  no operation moved by 1% of the time
where the time goes in v5:
time: 94.1 us; the launch traced here: 94 us
  Pallas kernels  92.8 us (99%)
  local copies, waits for them, and re-layouts  1.19 us (1%)
    pallas_call x1, Pallas kernels, body(): pl.pallas_call(functools.partial(kernel, d, nsub, t), out_shape=jax.Shape...  92.8 us

profile of v5, /device:TPU:1, one launch (start us, length us, event | category | flops | bytes accessed | tf_op | source)
XLA Modules:
  0.0 94.0 jit_solution(4644078464512828689)
XLA Ops:
  0.0 92.8 %shard_map.73 = f32[1,32]{1,0:T(1,128)} custom-call(s32[16,16]{1,0:T(8,128)} %mask_hbm.1, s32[16]{0:T(128)} %owner_hbm.1, s32[8]{0:T(128)} %ooff_hbm.1, s32[8]{0:T(128)} %voff_hbm.1, bf16[1,2048,128]{2,1,0:T(8,128)(2,1)} %b_hbm.1, bf16[32,128]{1,0:T(8,128)(2,1)} %ot_ref.1, bf16[32,128]{1,0:T(8,128)(2,1)} %vt_ref.1), custom_call_target="tpu_custom_call" | custom-call | tf_op jit(solution)/shard_map/pallas_call | solution.py:419
  92.8 1.2 %copy.9 = f32[1,32]{1,0:T(1,128)} copy(f32[1,32]{1,0:T(1,128)} %shard_map.73) | data formatting | bytes 256
